TPU v7x, 32 devices: a whole 2x2x4 slice. The times are simulated.
32 devices in a mesh: dp: 8 (over y, x, core), tensor: 4 (over z).
Axes of the slice: x: 2, y: 2, z: 4, core: 2. Of those that a mesh axis runs over, the one named last changes fastest.
Arguments:
- tokens: bfloat16 [16384, 768], P('dp'), may hold values from -6 to 6
- teacher: bfloat16 [16384, 768], P('dp'), may hold values from -6 to 6
- segment_ids: int32 [32, 512], P('dp'), may hold values from 0 to 7, never falling along the last dimension, each value on 1 to 256 neighbouring positions
- qkv_latent: bfloat16 [2, 768, 3, 768], P(None, 'dp', None, 'tensor'), may hold values from -1.5 to 1.5
- qv_bias: float32 [2, 768], P(None, 'tensor'), may hold values from -3 to 3
- proj_latent: bfloat16 [2, 768, 768], P(None, 'tensor', 'dp'), may hold values from -1.5 to 1.5
- proj_bias: float32 [768], replicated, may hold values from -3 to 3
- up_latent: bfloat16 [2, 768, 3072], P(None, 'dp', 'tensor'), may hold values from -1.5 to 1.5
- up_bias: float32 [3072], P('tensor'), may hold values from -3 to 3
- down_latent: bfloat16 [2, 3072, 768], P(None, 'tensor', 'dp'), may hold values from -1.5 to 1.5
- down_bias: float32 [768], replicated, may hold values from -3 to 3
- norm_gain: float32 [2, 768], replicated, may hold values from 0.5 to 1.5
- norm_shift: float32 [2, 768], replicated, may hold values from -3 to 3
- clip_bounds: float32 [4], replicated, may hold values from 1 to 3, as said below
- binary_scales: float32 [6, 2], replicated, as said below
Outputs:
- block_out: bfloat16 [16384, 768], P('dp')
- input_grad: float32 [16384, 768], P('dp')
- qkv_grad: float32 [2, 768, 3, 768], P(None, 'dp', None, 'tensor')
- qv_bias_grad: float32 [2, 768], P(None, 'tensor')
- proj_grad: float32 [2, 768, 768], P(None, 'tensor', 'dp')
- proj_bias_grad: float32 [768], replicated
- up_grad: float32 [2, 768, 3072], P(None, 'dp', 'tensor')
- up_bias_grad: float32 [3072], P('tensor')
- down_grad: float32 [2, 3072, 768], P(None, 'tensor', 'dp')
- down_bias_grad: float32 [768], replicated
- gain_grad: float32 [2, 768], replicated
- shift_grad: float32 [2, 768], replicated
- clip_grad: float32 [4], replicated
- scale_grad: float32 [6, 2], replicated
Inputs may be any that keep to these rules, and one draw needn't show every extreme that they name: `segment_ids`: within each packed sequence the ids never fall and run through 0 to 7; every document has 1 to 256 tokens and some document has exactly 256. `binary_scales`: every scale is positive. `clip_bounds`: every bound is positive.
All inputs are finite; a program needn't handle non-finite values.
Results may differ from a plain program's by a relative error of at most 0.019.
Values may be sent and summed in bfloat16 or wider, within the bound.
A program may use at most 192 MiB of HBM per device.

v0:
```python
import jax
import jax.numpy as jnp
from jax import lax
from jax.sharding import PartitionSpec as P

HEAD_DIM = 64


def squash(values, clip_at):
    ratio = values / clip_at
    bent = jnp.tanh(ratio)
    return (clip_at * bent, bent, ratio)


def squash_back(gradient, bent, ratio):
    slope = 1.0 - bent * bent
    return (gradient * slope, jnp.sum(gradient * (bent - ratio * slope)))


def binarize(latent, scale_first, scale_second):
    sign_vals = jnp.sign(latent).astype(jnp.float32)
    return (scale_first * sign_vals[0] + scale_second * sign_vals[1]).astype(jnp.bfloat16)


def norm_parts(values, gain, shift):
    centre = values - jnp.mean(values, axis=-1, keepdims=True)
    scale_inv = lax.rsqrt(jnp.mean(centre * centre, axis=-1, keepdims=True) + 1e-12)
    normed = centre * scale_inv
    return (normed * gain + shift, normed, scale_inv)


def norm_back(gradient, normed, scale_inv, gain):
    scaled = gradient * gain
    return scale_inv * (
        scaled
        - jnp.mean(scaled, axis=-1, keepdims=True)
        - normed * jnp.mean(scaled * normed, axis=-1, keepdims=True)
    )


def exact_gelu(values):
    return jax.nn.gelu(values, approximate=False)


def latent_grad(gradient, latent, scale_first, scale_second):
    keep_mask = jnp.abs(latent) < 1.0
    return jnp.stack(
        [
            jnp.where(keep_mask[0], gradient * scale_first, 0.0),
            jnp.where(keep_mask[1], gradient * scale_second, 0.0),
        ]
    )


def scale_part(gradient, latent, sum_axes):
    return jnp.sum(gradient[None] * jnp.sign(latent).astype(jnp.float32), axis=sum_axes)


def shards(
    tokens,
    teacher,
    segment_ids,
    qkv_latent,
    qv_bias,
    proj_latent,
    proj_bias,
    up_latent,
    up_bias,
    down_latent,
    down_bias,
    norm_gain,
    norm_shift,
    clip_bounds,
    binary_scales,
):
    qkv_full, proj_full, up_full, down_full = (
        lax.all_gather(qkv_latent, "dp", axis=1, tiled=True),
        lax.all_gather(proj_latent, "dp", axis=2, tiled=True),
        lax.all_gather(up_latent, "dp", axis=1, tiled=True),
        lax.all_gather(down_latent, "dp", axis=2, tiled=True),
    )
    head_cols = qkv_latent.shape[3]
    model_cols = tokens.shape[1]
    tok_rows = tokens.shape[0]
    seq_count = segment_ids.shape[0]
    seq_length = segment_ids.shape[1]
    local_heads = head_cols // HEAD_DIM
    qkv_first = binary_scales[0:3, 0][:, None]
    qkv_second = binary_scales[0:3, 1][:, None]
    w_qkv = binarize(qkv_full, qkv_first, qkv_second).reshape(model_cols, 3 * head_cols)
    w_proj = binarize(proj_full, binary_scales[3, 0], binary_scales[3, 1])
    w_up = binarize(up_full, binary_scales[4, 0], binary_scales[4, 1])
    w_down = binarize(down_full, binary_scales[5, 0], binary_scales[5, 1])
    inputs = tokens.astype(jnp.float32)
    act_one_full, bent_zero, ratio_zero = squash(inputs, clip_bounds[0])
    act_one = act_one_full.astype(jnp.bfloat16)
    bias_rows = jnp.concatenate([qv_bias[0], jnp.zeros_like(qv_bias[0]), qv_bias[1]])
    qkv_all = (jnp.dot(act_one, w_qkv, preferred_element_type=jnp.float32) + bias_rows).astype(
        jnp.bfloat16
    )
    shaped = qkv_all.reshape(seq_count, seq_length, 3, local_heads, HEAD_DIM)
    queries = shaped[:, :, 0]
    key_heads = shaped[:, :, 1]
    values = shaped[:, :, 2]
    same_doc = (segment_ids[:, :, None] == segment_ids[:, None, :])[:, None]
    factor = HEAD_DIM ** (-0.5)

    def score_block(query_part, key_part):
        raw_scores = (
            jnp.einsum("nqhe,nkhe->nhqk", query_part, key_part, preferred_element_type=jnp.float32)
            * factor
        )
        return jnp.where(same_doc, raw_scores, -1000000000.0)

    scores = score_block(queries, key_heads)
    row_top = jnp.max(scores, axis=-1, keepdims=True)
    exp_terms = jnp.exp(scores - row_top)
    row_total = jnp.sum(exp_terms, axis=-1, keepdims=True)
    prob_rows = exp_terms / row_total
    log_total = row_top + jnp.log(row_total)
    context = jnp.einsum(
        "nhqk,nkhe->nqhe",
        prob_rows.astype(jnp.bfloat16),
        values,
        preferred_element_type=jnp.float32,
    ).reshape(tok_rows, head_cols)
    act_two_full, bent_one, ratio_one = squash(context, clip_bounds[1])
    act_two = act_two_full.astype(jnp.bfloat16)
    attention = (
        lax.psum(
            jnp.dot(act_two, w_proj, preferred_element_type=jnp.float32).astype(jnp.bfloat16),
            "tensor",
        ).astype(jnp.float32)
        + proj_bias
    )
    h_one, normed_one, inv_one = norm_parts(inputs + attention, norm_gain[0], norm_shift[0])
    act_three_full, bent_two, ratio_two = squash(h_one, clip_bounds[2])
    act_three = act_three_full.astype(jnp.bfloat16)
    hidden = jnp.dot(act_three, w_up, preferred_element_type=jnp.float32) + up_bias
    activated, gelu_back = jax.vjp(exact_gelu, hidden)
    act_four_full, bent_three, ratio_three = squash(activated, clip_bounds[3])
    act_four = act_four_full.astype(jnp.bfloat16)
    feed_out = (
        lax.psum(
            jnp.dot(act_four, w_down, preferred_element_type=jnp.float32).astype(jnp.bfloat16),
            "tensor",
        ).astype(jnp.float32)
        + down_bias
    )
    y_full, normed_two, inv_two = norm_parts(h_one + feed_out, norm_gain[1], norm_shift[1])
    block_out = y_full.astype(jnp.bfloat16)
    out_grad = y_full - teacher.astype(jnp.float32)
    gain_two = jnp.sum(out_grad * normed_two, axis=0)
    shift_two = jnp.sum(out_grad, axis=0)
    grad_two = norm_back(out_grad, normed_two, inv_two, norm_gain[1])
    down_bias_part = jnp.sum(grad_two, axis=0)
    grad_two_low = grad_two.astype(jnp.bfloat16)
    down_weight_grad = jnp.einsum(
        "ru,rd->ud", act_four, grad_two_low, preferred_element_type=jnp.float32
    )
    grad_four = jnp.einsum("rd,ud->ru", grad_two_low, w_down, preferred_element_type=jnp.float32)
    grad_act_four, clip_three = squash_back(grad_four, bent_three, ratio_three)
    grad_hidden = gelu_back(grad_act_four)[0].astype(jnp.bfloat16)
    up_bias_part = jnp.sum(grad_hidden.astype(jnp.float32), axis=0)
    up_weight_grad = jnp.einsum(
        "rd,ru->du", act_three, grad_hidden, preferred_element_type=jnp.float32
    )
    grad_three = lax.psum(
        jnp.einsum("ru,du->rd", grad_hidden, w_up, preferred_element_type=jnp.float32).astype(
            jnp.bfloat16
        ),
        "tensor",
    ).astype(jnp.float32)
    grad_three_in, clip_two = squash_back(grad_three, bent_two, ratio_two)
    grad_h = grad_two + grad_three_in
    gain_one = jnp.sum(grad_h * normed_one, axis=0)
    shift_one = jnp.sum(grad_h, axis=0)
    grad_one = norm_back(grad_h, normed_one, inv_one, norm_gain[0])
    proj_bias_part = jnp.sum(grad_one, axis=0)
    grad_one_low = grad_one.astype(jnp.bfloat16)
    proj_weight_grad = jnp.einsum(
        "rc,rd->cd", act_two, grad_one_low, preferred_element_type=jnp.float32
    )
    grad_context_raw = jnp.einsum(
        "rd,cd->rc", grad_one_low, w_proj, preferred_element_type=jnp.float32
    )
    grad_context_full, clip_one = squash_back(grad_context_raw, bent_one, ratio_one)
    grad_context = grad_context_full.astype(jnp.bfloat16).reshape(
        seq_count, seq_length, local_heads, HEAD_DIM
    )
    scores = score_block(queries, key_heads)
    prob_rows = jnp.exp(scores - log_total)
    grad_values = jnp.einsum(
        "nhqk,nqhe->nkhe",
        prob_rows.astype(jnp.bfloat16),
        grad_context,
        preferred_element_type=jnp.float32,
    )
    grad_probs = jnp.einsum(
        "nqhe,nkhe->nhqk", grad_context, values, preferred_element_type=jnp.float32
    )
    grad_scores = (
        prob_rows * (grad_probs - jnp.sum(prob_rows * grad_probs, axis=-1, keepdims=True))
    ).astype(jnp.bfloat16)
    grad_queries = (
        jnp.einsum("nhqk,nkhe->nqhe", grad_scores, key_heads, preferred_element_type=jnp.float32)
        * factor
    )
    grad_keys = (
        jnp.einsum("nhqk,nqhe->nkhe", grad_scores, queries, preferred_element_type=jnp.float32)
        * factor
    )
    grad_qkv = (
        jnp.stack([grad_queries, grad_keys, grad_values], axis=2)
        .astype(jnp.bfloat16)
        .reshape(tok_rows, 3 * head_cols)
    )
    bias_sums = jnp.sum(grad_qkv.astype(jnp.float32), axis=0).reshape(3, head_cols)
    qv_part = jnp.stack([bias_sums[0], bias_sums[2]])
    qkv_weight_grad = jnp.einsum(
        "rd,rc->dc", act_one, grad_qkv, preferred_element_type=jnp.float32
    ).reshape(model_cols, 3, head_cols)
    grad_act_one = lax.psum(
        jnp.einsum("rc,dc->rd", grad_qkv, w_qkv, preferred_element_type=jnp.float32).astype(
            jnp.bfloat16
        ),
        "tensor",
    ).astype(jnp.float32)
    grad_inputs, clip_zero = squash_back(grad_act_one, bent_zero, ratio_zero)
    input_grad = grad_one + grad_inputs
    qkv_terms = latent_grad(qkv_weight_grad, qkv_full, qkv_first, qkv_second)
    proj_terms = latent_grad(proj_weight_grad, proj_full, binary_scales[3, 0], binary_scales[3, 1])
    up_terms = latent_grad(up_weight_grad, up_full, binary_scales[4, 0], binary_scales[4, 1])
    down_terms = latent_grad(down_weight_grad, down_full, binary_scales[5, 0], binary_scales[5, 1])
    scale_parts = jnp.concatenate(
        [
            scale_part(qkv_weight_grad, qkv_full, (1, 3)).T,
            scale_part(proj_weight_grad, proj_full, (1, 2))[None],
            scale_part(up_weight_grad, up_full, (1, 2))[None],
            scale_part(down_weight_grad, down_full, (1, 2))[None],
        ],
        axis=0,
    )
    qkv_grad, proj_grad, up_grad, down_grad = (
        lax.psum_scatter(qkv_terms, "dp", scatter_dimension=1, tiled=True),
        lax.psum_scatter(proj_terms, "dp", scatter_dimension=2, tiled=True),
        lax.psum_scatter(up_terms, "dp", scatter_dimension=1, tiled=True),
        lax.psum_scatter(down_terms, "dp", scatter_dimension=2, tiled=True),
    )
    qv_bias_grad, proj_bias_grad, up_bias_grad, down_bias_grad, gain_grad, shift_grad, clip_even = (
        lax.psum(
            (
                qv_part,
                proj_bias_part,
                up_bias_part,
                down_bias_part,
                jnp.stack([gain_one, gain_two]),
                jnp.stack([shift_one, shift_two]),
                jnp.stack([clip_zero, clip_two]),
            ),
            "dp",
        )
    )
    scale_grad, clip_odd = lax.psum(
        (scale_parts, jnp.stack([clip_one, clip_three])), ("dp", "tensor")
    )
    clip_grad = jnp.stack([clip_even[0], clip_odd[0], clip_even[1], clip_odd[1]])
    return (
        block_out,
        input_grad,
        qkv_grad,
        qv_bias_grad,
        proj_grad,
        proj_bias_grad,
        up_grad,
        up_bias_grad,
        down_grad,
        down_bias_grad,
        gain_grad,
        shift_grad,
        clip_grad,
        scale_grad,
    )


def solution(mesh):
    return jax.shard_map(
        shards,
        mesh=mesh,
        in_specs=(
            P("dp", None),
            P("dp", None),
            P("dp", None),
            P(None, "dp", None, "tensor"),
            P(None, "tensor"),
            P(None, "tensor", "dp"),
            P(),
            P(None, "dp", "tensor"),
            P("tensor"),
            P(None, "tensor", "dp"),
            P(),
            P(),
            P(),
            P(),
            P(),
        ),
        out_specs=(
            P("dp", None),
            P("dp", None),
            P(None, "dp", None, "tensor"),
            P(None, "tensor"),
            P(None, "tensor", "dp"),
            P(),
            P(None, "dp", "tensor"),
            P("tensor"),
            P(None, "tensor", "dp"),
            P(),
            P(),
            P(),
            P(),
            P(),
        ),
        check_vma=False,
    )
```

profile of v0, /device:TPU:0, one launch (start us, length us, event | category | flops | bytes accessed | tf_op | source)
XLA Modules:
  0.0 910.5 jit_solution(15919581920457590564)
XLA Ops:
  20.2 12.7 %all_gather.13 = bf16[2,192,768]{1,0,2:T(2,128)(2,1)S(1)} all-gather(bf16[2,192,96]{1,0,2:T(2,128)(2,1)S(1)} %copy.99), channel_id=1, replica_groups=mesh['dp'=8,'tensor'=4] {'dp'}, dimensions={2}, use_global_device_ids=true | all-gather | bytes 663552 | tf_op jit(solution)/shard_map/all_gather | solution.py:78
  35.2 7.2 all-gather.4.cloned.1.call-done
  42.4 5.6 copy.93
  52.0 4.1 add_convert_fusion.1
  56.1 6.2 reshape.180
  64.7 4.4 fusion.64
  73.7 3.3 fusion.39
  81.6 6.8 copy.102
  88.4 16.2 %all-gather.6.cloned.1.call-done = bf16[2,768,768]{2,1,0:T(8,128)(2,1)} async-done(((bf16[2,96,768]{2,1,0:T(8,128)(2,1)}), bf16[2,768,768]{2,1,0:T(8,128)(2,1)}) %all-gather.6.cloned.1.call-update) | async-done | bytes 2359312 | tf_op jit(solution)/shard_map/all_gather | solution.py:79
  113.1 115.3 %all-reduce.9.cloned.1.call-done = bf16[2048,768]{1,0:T(8,128)(2,1)} async-done(((bf16[2048,768]{1,0:T(8,128)(2,1)}), bf16[2048,768]{1,0:T(8,128)(2,1)}) %all-reduce.9.cloned.1.call-update) | async-done | bytes 3145744 | tf_op jit(solution)/shard_map/psum | solution.py:130
  228.5 3.1 fusion.19
  233.9 19.0 %fusion.6 = (f32[2048,768]{1,0:T(8,128)S(1)}, f32[2048,768]{1,0:T(8,128)S(1)}) fusion(f32[768]{0:T(1024)S(1)} %copy-done.45, bf16[768,768]{1,0:T(8,128)(2,1)S(1)} %copy-done.28, f32[]{:T(128)} %bitcast.16, f32[768]{0:T(1024)S(1)} %get-tuple-element.82, f32[768]{0:T(1024)S(1)} %get-tuple-element.148, f32[2048]{0:T(1024)S(1)} %add_rsqrt_fusion.1, ...), kind=kOutput, calls=%fused_computation.19 | convolution fusion | flops 2532311040 | bytes 20082692 | tf_op jit(solution)/shard_map/dot_general | solution.py:139
  257.5 5.2 convolution_convert_fusion.1
  262.9 120.2 %all-reduce.11.cloned.1.call-done = bf16[2048,768]{1,0:T(8,128)(2,1)} async-done(((bf16[2048,768]{1,0:T(8,128)(2,1)}), bf16[2048,768]{1,0:T(8,128)(2,1)}) %all-reduce.11.cloned.1.call-update) | async-done | bytes 3145744 | tf_op jit(solution)/shard_map/psum | solution.py:144
  383.0 5.1 fusion.50
  388.2 3.9 multiply_reduce_fusion.6
  392.1 7.2 fusion.18
  399.3 4.4 fusion.54
  403.8 12.2 %convert_reduce_fusion = (f32[768]{0:T(1024)S(1)}, bf16[2048,768]{1,0:T(8,128)(2,1)S(1)}, f32[]{:T(128)}) fusion(f32[2048,768]{1,0:T(8,128)S(1)} %bitcast.175, f32[]{:T(128)} %bitcast.15, f32[2048,768]{1,0:T(8,128)} %copy-done.49, f32[768]{0:T(1024)S(1)} %copy-done.45, bf16[768,768]{1,0:T(8,128)(2,1)S(1)} %copy-done.31, f32[2048,768]{1,0:T(8,128)S(1)} %get-tuple-element.93), kind=kOutput, calls=%fused_computation.24 | convolution fusion | flops 2458385664 | bytes 23205896 | tf_op jit(solution)/shard_map/rd,ud->ru/dot_general | solution.py:161
  417.6 4.0 convolution_convert_fusion
  428.8 8.7 fusion.30
  443.3 8.2 copy.113
  451.6 90.2 %all-reduce.13.cloned.1.call-done = bf16[2048,768]{1,0:T(8,128)(2,1)} async-done(((bf16[2048,768]{1,0:T(8,128)(2,1)}), bf16[2048,768]{1,0:T(8,128)(2,1)}) %all-reduce.13.cloned.1.call-update) | async-done | bytes 3145744 | tf_op jit(solution)/shard_map/psum | solution.py:168
  541.9 12.7 %multiply_reduce_fusion.3 = (f32[768]{0:T(1024)S(1)}, f32[2048]{0:T(1024)S(1)}, f32[]{:T(128)}, f32[2048]{0:T(1024)S(1)}, f32[768]{0:T(1024)S(1)}, /*index=5*/f32[2048,768]{1,0:T(8,128)S(1)}) fusion(f32[2048]{0:T(1024)S(1)} %add_rsqrt_fusion.1, f32[2048]{0:T(1024)S(1)} %broadcast_multiply_fusion.5, f32[768]{0:T(1024)S(1)} %copy-done.33, ...), kind=kLoop, calls=%fused_computation.23 | loop fusion | flops 39315968 | bytes 22068232 | tf_op jit(solution)/shard_map/reduce_sum | solution.py:176
  554.5 3.0 fusion.55
  560.4 2.9 multiply_reduce_fusion.13
  563.3 3.0 reshape.181
  569.9 3.5 copy.125
  573.4 3.3 reshape.185
  576.7 8.6 multiply_reduce_fusion
  585.3 7.1 multiply_convert_fusion
  597.2 5.1 multiply_bitcast_fusion
  602.3 6.7 fusion.34
  613.5 4.1 convolution_convert_fusion.2
  619.7 4.4 fusion.51
  627.8 7.0 copy.123
  634.8 8.0 reshape.183
  645.4 7.1 fusion.40
  659.6 4.0 multiply_reduce_fusion.10
  663.7 4.0 multiply_reduce_fusion.11
  673.0 3.2 multiply_reduce_fusion.12
  678.3 44.3 %all-reduce.1 = (f32[2]{0:T(128)S(1)}, f32[6,2]{0,1:T(2,128)}) all-reduce(f32[2]{0:T(128)S(1)} %pad_maximum_fusion.10, f32[6,2]{0,1:T(2,128)S(1)} %pad_maximum_fusion.8), channel_id=1, replica_groups=mesh['dp'=8,'tensor'=4] {'dp','tensor'}, use_global_device_ids=true, to_apply=%region_38.39 | all-reduce | flops 14 | bytes 112 | tf_op jit(solution)/shard_map/psum | solution.py:264
  725.3 70.0 %all-reduce.15.cloned.1.call-done = bf16[2048,768]{1,0:T(8,128)(2,1)} async-done(((bf16[2048,768]{1,0:T(8,128)(2,1)}), bf16[2048,768]{1,0:T(8,128)(2,1)}) %all-reduce.15.cloned.1.call-update) | async-done | bytes 3145744 | tf_op jit(solution)/shard_map/psum | solution.py:223
  795.3 7.9 fusion.5
  804.6 25.0 %all-reduce.2 = (f32[2,192]{1,0:T(2,128)}, f32[768]{0:T(1024)}, f32[768]{0:T(1024)}, f32[768]{0:T(1024)}, f32[2,768]{1,0:T(2,128)}, /*index=5*/f32[2,768]{1,0:T(2,128)}, f32[2]{0:T(128)S(1)}) all-reduce(f32[2,192]{1,0:T(2,128)S(1)} %pad_maximum_fusion.7, f32[768]{0:T(1024)S(1)} %get-tuple-element.96, ...), channel_id=1, replica_groups=mesh['dp'=8,'tensor'=4] {'dp'}, use_global_device_ids=true, to_apply=%region_17.18 | all-reduce | flops 5762 | bytes 46096 | tf_op jit(solution)/shard_map/psum | solution.py:251
  830.3 3.1 pad_maximum_fusion.11
  833.3 12.4 %reduce-scatter.10.cloned.1.call-done = f32[96,1152]{1,0:T(8,128)} async-done(((f32[768,1152]{1,0:T(8,128)}), f32[96,1152]{1,0:T(8,128)}) %reduce-scatter.10.cloned.1.call-update) | async-done | bytes 442384
  848.3 55.2 %reduce-scatter.8.cloned.1.call-done = f32[2,96,768]{2,1,0:T(8,128)} async-done(((f32[2,768,768]{2,1,0:T(8,128)}), f32[2,96,768]{2,1,0:T(8,128)}) %reduce-scatter.8.cloned.1.call-update) | async-done | bytes 589840 | tf_op jit(solution)/shard_map/reduce_scatter | solution.py:247
  (216 shorter events, 105.8 us)
Async XLA Ops:
  7.2 35.2 %all-gather.4.cloned.1.call-start = ((), (), s32[]{:S(2)}) async-start(), calls=%async_computation.3 | async-start | bytes 2654208 | tf_op jit(solution)/shard_map/all_gather | solution.py:77
  9.2 72.3 %all-gather.8.cloned.1.call-start = ((), (), s32[]{:S(2)}) async-start(), calls=%async_computation.6 | async-start | bytes 2654208 | tf_op jit(solution)/shard_map/all_gather | solution.py:80
  11.3 93.3 %all-gather.6.cloned.1.call-start = ((), (), s32[]{:S(2)}) async-start(), calls=%async_computation.5 | async-start | bytes 2654208 | tf_op jit(solution)/shard_map/all_gather | solution.py:79
  12.0 216.4 %all-reduce.9.cloned.1.call-start = ((), (), s32[]{:S(2)}) async-start(), calls=%async_computation.4 | async-start | bytes 6291456 | tf_op jit(solution)/shard_map/psum | solution.py:130
  12.8 36.9 %copy-start.39 = (f32[3]{0:T(128)}, f32[3]{0:T(128)S(1)}, u32[]{:S(2)}) copy-start(f32[3]{0:T(128)S(1)} %get-tuple-element.132) | copy-start | bytes 40
  12.8 36.9 %copy-start.41 = (f32[3]{0:T(128)}, f32[3]{0:T(128)S(1)}, u32[]{:S(2)}) copy-start(f32[3]{0:T(128)S(1)} %get-tuple-element.133) | copy-start | bytes 40
  35.2 43.4 %copy-start.25 = (bf16[192,768]{1,0:T(8,128)(2,1)}, bf16[192,768]{1,0:T(8,128)(2,1)S(1)}, u32[]{:S(2)}) copy-start(bf16[192,768]{1,0:T(8,128)(2,1)S(1)} %fusion.49) | copy-start | bytes 884740
  64.7 4.4 copy-start.20
  64.7 4.4 copy-start.22
  64.7 6.3 copy-start.21
  69.1 4.6 copy-start
  71.0 6.0 copy-start.34
  78.5 3.0 copy-start.43
  81.4 301.6 %all-reduce.11.cloned.1.call-start = ((), (), s32[]{:S(2)}) async-start(), calls=%async_computation.7 | async-start | bytes 6291456 | tf_op jit(solution)/shard_map/psum | solution.py:144
  104.6 5.2 copy-start.7
  109.8 118.7 %copy-start.33 = (f32[768]{0:T(1024)S(1)}, f32[768]{0:T(1024)}, u32[]{:S(2)}) copy-start(f32[768]{0:T(1024)} %param.21) | copy-start | bytes 9220
  113.1 120.7 %copy-start.45 = (f32[768]{0:T(1024)S(1)}, f32[768]{0:T(1024)}, u32[]{:S(2)}) copy-start(f32[768]{0:T(1024)} %param.23) | copy-start | bytes 9220
  228.4 3.1 copy-start.2
  228.5 5.4 copy-start.28
  233.8 23.7 %copy-start.30 = (bf16[768,768]{1,0:T(8,128)(2,1)S(1)}, bf16[768,768]{1,0:T(8,128)(2,1)}, u32[]{:S(2)}) copy-start(bf16[768,768]{1,0:T(8,128)(2,1)} %fusion.38) | copy-start | bytes 3538948
  252.9 4.7 copy-start.49
  257.5 125.5 %copy-start.35 = (f32[768]{0:T(1024)S(1)}, f32[768]{0:T(1024)}, u32[]{:S(2)}) copy-start(f32[768]{0:T(1024)} %param.25) | copy-start | bytes 9220
  262.8 279.1 %all-reduce.13.cloned.1.call-start = ((), (), s32[]{:S(2)}) async-start(), calls=%async_computation.8 | async-start | bytes 6291456 | tf_op jit(solution)/shard_map/psum | solution.py:168
  383.0 5.2 copy-start.3
  383.0 5.2 copy-start.10
  388.1 4.0 copy-start.13
  388.2 15.6 %slice-start = ((s8[6291456]{0:T(1024)(128)(4,1)}), s8[4194304]{0:T(1024)(128)(4,1)S(1)}, s32[]{:S(2)}) async-start(s8[6291456]{0:T(1024)(128)(4,1)} %bitcast.174), calls=%async_computation.14 | async-start | bytes 8388608
  392.1 11.6 %slice-start.1 = ((s8[6291456]{0:T(1024)(128)(4,1)}), s8[2097152]{0:T(1024)(128)(4,1)S(1)}, s32[]{:S(2)}) async-start(s8[6291456]{0:T(1024)(128)(4,1)} %bitcast.174), calls=%async_computation.15 | async-start | bytes 4194304
  399.3 4.4 copy-start.31
  403.7 12.3 %copy-start.11 = (f32[2048,768]{1,0:T(8,128)}, f32[2048,768]{1,0:T(8,128)S(1)}, u32[]{:S(2)}) copy-start(f32[2048,768]{1,0:T(8,128)S(1)} %get-tuple-element.93) | copy-start | bytes 18874372
  403.8 13.9 %copy-start.29 = (bf16[768,768]{1,0:T(8,128)(2,1)S(1)}, bf16[768,768]{1,0:T(8,128)(2,1)}, u32[]{:S(2)}) copy-start(bf16[768,768]{1,0:T(8,128)(2,1)} %fusion.37) | copy-start | bytes 3538948
  421.7 246.2 %all-reduce.17.cloned.1.call-start = ((), (), s32[]{:S(2)}) async-start(), calls=%async_computation.13 | async-start | bytes 9437184
  421.7 6.4 copy-start.8
  451.6 271.8 %reduce-scatter.12.cloned.1.call-start = ((), (), s32[]{:S(2)}) async-start(), calls=%async_computation.12 | async-start | bytes 1327104
  541.9 12.7 %copy-start.4 = (bf16[2048,768]{1,0:T(8,128)(2,1)S(1)}, bf16[2048,768]{1,0:T(8,128)(2,1)}, u32[]{:S(2)}) copy-start(bf16[2048,768]{1,0:T(8,128)(2,1)} %all-reduce.9.cloned.1.call-done) | copy-start | bytes 9437188
  557.5 5.8 copy-start.5
  585.3 9.9 %copy-start.23 = (bf16[4,512,1,3,64]{1,0,4,3,2:T(4,128)(2,1)S(1)}, bf16[4,512,1,3,64]{1,0,4,3,2:T(4,128)(2,1)}, u32[]{:S(2)}) copy-start(bf16[4,512,1,3,64]{1,0,4,3,2:T(4,128)(2,1)} %copy-done.22) | copy-start | bytes 2359300
  597.2 198.2 %all-reduce.15.cloned.1.call-start = ((), (), s32[]{:S(2)}) async-start(), calls=%async_computation.9 | async-start | bytes 6291456 | tf_op jit(solution)/shard_map/psum | solution.py:223
  597.2 5.1 copy-start.17
  602.3 6.7 copy-start.24
  609.0 4.4 copy-start.32
  617.6 228.2 %reduce-scatter.10.cloned.1.call-start = ((), (), s32[]{:S(2)}) async-start(), calls=%async_computation.11 | async-start | bytes 3981312
  619.6 5.6 copy-start.40
  619.7 5.6 copy-start.42
  642.9 260.6 %reduce-scatter.8.cloned.1.call-start = ((), (), s32[]{:S(2)}) async-start(), calls=%async_computation.10 | async-start | bytes 5308416 | tf_op jit(solution)/shard_map/reduce_scatter | solution.py:247
  658.3 9.5 %copy-start.37 = (f32[768]{0:T(1024)S(1)}, f32[768]{0:T(1024)}, u32[]{:S(2)}) copy-start(f32[768]{0:T(1024)} %get-tuple-element.72) | copy-start | bytes 9220
  658.3 9.5 %copy-start.36 = (f32[768]{0:T(1024)S(1)}, f32[768]{0:T(1024)}, u32[]{:S(2)}) copy-start(f32[768]{0:T(1024)} %get-tuple-element.73) | copy-start | bytes 9220
  725.3 79.3 %copy-start.38 = (f32[768]{0:T(1024)S(1)}, f32[768]{0:T(1024)}, u32[]{:S(2)}) copy-start(f32[768]{0:T(1024)} %get-tuple-element.92) | copy-start | bytes 9220
  (15 other events, 30.4 us)
Sparse Core Ops, SparseCore 0:
  10.4 31.8 all-gather.3
  44.8 28.8 all-gather.7
  75.7 28.8 all-gather.5
  107.4 121.0 all-reduce.8
  262.9 120.0 all-reduce.10
  421.8 120.0 all-reduce.12
  545.2 85.5 all-reduce.16
  634.1 36.7 reduce-scatter.11
  673.2 122.0 all-reduce.14
  798.7 47.0 reduce-scatter.9
  849.8 53.7 reduce-scatter.7
where the time goes:
time: 921 us; the launch traced here: 910 us
  waiting for transfers between devices  488 us (53%)
  other arithmetic  116 us (13%)
  matrix products  107 us (12%)
  local copies, waits for them, and re-layouts  102 us (11%)
  blocking collectives  82 us (9%)
  between operations  15.8 us (2%)
    psum x1, waiting for transfers between devices, shards(): lax.psum(jnp.dot(act_four, w_down, preferred_element_type=jnp.float32).as...  120 us
    psum x1, waiting for transfers between devices, shards(): lax.psum(jnp.dot(act_two, w_proj, preferred_element_type=jnp.float32).ast...  115 us
    psum x1, waiting for transfers between devices, shards(): lax.psum(jnp.einsum('ru,du->rd', grad_hidden, w_up, preferred_element_typ...  90.2 us
    psum x1, waiting for transfers between devices, shards(): lax.psum(jnp.einsum('rc,dc->rd', grad_qkv, w_qkv, preferred_element_type=...  70 us
    unnamed x121, local copies, waits for them, and re-layouts  57.3 us
    reduce_scatter x1, waiting for transfers between devices, shards(): lax.psum_scatter(up_terms, 'dp', scatter_dimension=1, tiled=True)  55.2 us
    psum x1, blocking collectives, shards(): lax.psum((scale_parts, jnp.stack([clip_one, clip_three])), ('dp', 'tensor'))  44.3 us
    psum x1, blocking collectives, shards(): lax.psum((qv_part, proj_bias_part, up_bias_part, down_bias_part, jnp.stac...  25 us
  transfers between devices with their start and end apart: 11, of which 8 were waited for; matrix products, arithmetic and copies ran while one was open for 26% of the time, Pallas kernels for 0%

commit v1 on v0

v1 whole, which is shorter than its diff:
```python
import jax
import jax.numpy as jnp
from jax import lax
from jax.sharding import PartitionSpec as P

HEAD_DIM = 64
F32 = jnp.float32
LOW = jnp.bfloat16


def dot_nn(a, b):
    return lax.dot_general(a, b, (((1,), (0,)), ((), ())), preferred_element_type=F32)


def dot_nt(a, b):
    return lax.dot_general(a, b, (((1,), (1,)), ((), ())), preferred_element_type=F32)


def dot_tn(a, b):
    return lax.dot_general(a, b, (((0,), (0,)), ((), ())), preferred_element_type=F32)


def squash(values, clip_at):
    ratio = values / clip_at
    bent = jnp.tanh(ratio)
    return (clip_at * bent, bent, ratio)


def squash_back(gradient, bent, ratio):
    slope = 1.0 - bent * bent
    return (gradient * slope, jnp.sum(gradient * (bent - ratio * slope)))


def norm_parts(values, gain, shift):
    centre = values - jnp.mean(values, axis=-1, keepdims=True)
    scale_inv = lax.rsqrt(jnp.mean(centre * centre, axis=-1, keepdims=True) + 1e-12)
    normed = centre * scale_inv
    return (normed * gain + shift, normed, scale_inv)


def norm_back(gradient, normed, scale_inv, gain):
    scaled = gradient * gain
    return scale_inv * (
        scaled
        - jnp.mean(scaled, axis=-1, keepdims=True)
        - normed * jnp.mean(scaled * normed, axis=-1, keepdims=True)
    )


def exact_gelu(values):
    return jax.nn.gelu(values, approximate=False)


def shards(
    tokens,
    teacher,
    segment_ids,
    qkv_latent,
    qv_bias,
    proj_latent,
    proj_bias,
    up_latent,
    up_bias,
    down_latent,
    down_bias,
    norm_gain,
    norm_shift,
    clip_bounds,
    binary_scales,
):
    groups = lax.axis_size("tensor")
    parts = lax.axis_size("dp")
    group = lax.axis_index("tensor")
    seqs = segment_ids.shape[0] // groups
    length = segment_ids.shape[1]
    rows = seqs * length
    model = tokens.shape[1]
    own_rows = qkv_latent.shape[1]
    head_cols = qkv_latent.shape[3]
    units = up_latent.shape[2]
    heads = head_cols // HEAD_DIM

    tokens = lax.dynamic_slice_in_dim(tokens, group * rows, rows, 0)
    teacher = lax.dynamic_slice_in_dim(teacher, group * rows, rows, 0)
    segment_ids = lax.dynamic_slice_in_dim(segment_ids, group * seqs, seqs, 0)

    latents = jnp.concatenate(
        [
            qkv_latent.reshape(2, own_rows, 3 * head_cols),
            proj_latent.transpose(0, 2, 1),
            up_latent,
            down_latent.transpose(0, 2, 1),
        ],
        axis=2,
    )
    widths = [head_cols] * 4 + [units] * 2
    scale_cols = jnp.concatenate(
        [jnp.broadcast_to(binary_scales[m][:, None], (2, w)) for m, w in enumerate(widths)], axis=1
    )
    signs = jnp.sign(latents).astype(F32)
    w_own = (scale_cols[0] * signs[0] + scale_cols[1] * signs[1]).astype(LOW)
    w_all = lax.all_gather(w_own, ("tensor", "dp"), axis=0, tiled=False)
    w_all = w_all.reshape(groups, model, 4 * head_cols + 2 * units)
    bias_all = lax.all_gather(
        jnp.concatenate([qv_bias[0], qv_bias[1], up_bias]), "tensor", axis=0, tiled=False
    )
    edge = 3 * head_cols

    inputs = tokens.astype(F32)
    act_one_full, bent_zero, ratio_zero = squash(inputs, clip_bounds[0])
    act_one = act_one_full.astype(LOW)
    same_doc = (segment_ids[:, :, None] == segment_ids[:, None, :])[:, None]
    factor = HEAD_DIM ** (-0.5)

    attention = jnp.zeros((rows, model), F32)
    kept = []
    for g in range(groups):
        w_qkv = w_all[g, :, :edge]
        bias = jnp.concatenate(
            [
                bias_all[g, :head_cols],
                jnp.zeros((head_cols,), F32),
                bias_all[g, head_cols : 2 * head_cols],
            ]
        )
        qkv = (dot_nn(act_one, w_qkv) + bias).astype(LOW).reshape(seqs, length, 3, heads, HEAD_DIM)
        q, k, v = qkv[:, :, 0], qkv[:, :, 1], qkv[:, :, 2]
        scores = jnp.einsum("nqhe,nkhe->nhqk", q, k, preferred_element_type=F32) * factor
        scores = jnp.where(same_doc, scores, -1000000000.0)
        top = jnp.max(scores, axis=-1, keepdims=True)
        terms = jnp.exp(scores - top)
        total = jnp.sum(terms, axis=-1, keepdims=True)
        probs = (terms / total).astype(LOW)
        context = jnp.einsum("nhqk,nkhe->nqhe", probs, v, preferred_element_type=F32).reshape(
            rows, head_cols
        )
        act_full, bent_one, ratio_one = squash(context, clip_bounds[1])
        act_two = act_full.astype(LOW)
        attention += dot_nt(act_two, w_all[g, :, edge : edge + head_cols]).astype(LOW).astype(F32)
        kept.append((q, k, v, probs, act_two, bent_one, ratio_one))
    h_one, normed_one, inv_one = norm_parts(inputs + (attention + proj_bias), norm_gain[0], norm_shift[0])
    act_three_full, bent_two, ratio_two = squash(h_one, clip_bounds[2])
    act_three = act_three_full.astype(LOW)

    feed = jnp.zeros((rows, model), F32)
    start_up = 4 * head_cols
    start_down = start_up + units
    kept_ffn = []
    for g in range(groups):
        hidden = dot_nn(act_three, w_all[g, :, start_up:start_down]) + bias_all[g, 2 * head_cols :]
        activated, gelu_back = jax.vjp(exact_gelu, hidden)
        act_full, bent_three, ratio_three = squash(activated, clip_bounds[3])
        act_four = act_full.astype(LOW)
        feed += dot_nt(act_four, w_all[g, :, start_down:]).astype(LOW).astype(F32)
        kept_ffn.append((act_four, gelu_back, bent_three, ratio_three))
    y_full, normed_two, inv_two = norm_parts(h_one + (feed + down_bias), norm_gain[1], norm_shift[1])
    block_out = lax.all_gather(y_full.astype(LOW), "tensor", axis=0, tiled=True)

    out_grad = y_full - teacher.astype(F32)
    gain_two = jnp.sum(out_grad * normed_two, axis=0)
    shift_two = jnp.sum(out_grad, axis=0)
    grad_two = norm_back(out_grad, normed_two, inv_two, norm_gain[1])
    down_bias_part = jnp.sum(grad_two, axis=0)
    grad_two_low = grad_two.astype(LOW)
    grads = [[] for _ in range(groups)]
    up_bias_part = []
    clip_three = 0.0
    grad_three = jnp.zeros((rows, model), F32)
    g_down, g_up = [], []
    for g in range(groups):
        act_four, gelu_back, bent_three, ratio_three = kept_ffn[g]
        g_down.append(dot_tn(grad_two_low, act_four).astype(LOW))
        grad_four = dot_nn(grad_two_low, w_all[g, :, start_down:])
        grad_act, clip_part = squash_back(grad_four, bent_three, ratio_three)
        clip_three += clip_part
        grad_hidden = gelu_back(grad_act)[0].astype(LOW)
        up_bias_part.append(jnp.sum(grad_hidden.astype(F32), axis=0))
        g_up.append(dot_tn(act_three, grad_hidden).astype(LOW))
        grad_three += dot_nt(grad_hidden, w_all[g, :, start_up:start_down]).astype(LOW).astype(F32)
    grad_three_in, clip_two = squash_back(grad_three, bent_two, ratio_two)
    grad_h = grad_two + grad_three_in
    gain_one = jnp.sum(grad_h * normed_one, axis=0)
    shift_one = jnp.sum(grad_h, axis=0)
    grad_one = norm_back(grad_h, normed_one, inv_one, norm_gain[0])
    proj_bias_part = jnp.sum(grad_one, axis=0)
    grad_one_low = grad_one.astype(LOW)

    clip_one = 0.0
    grad_act_one = jnp.zeros((rows, model), F32)
    g_att = []
    q_bias_part, v_bias_part = [], []
    for g in range(groups):
        q, k, v, probs, act_two, bent_one, ratio_one = kept[g]
        w_o = w_all[g, :, edge : edge + head_cols]
        g_proj = dot_tn(grad_one_low, act_two).astype(LOW)
        grad_ctx, clip_part = squash_back(dot_nn(grad_one_low, w_o), bent_one, ratio_one)
        clip_one += clip_part
        grad_ctx = grad_ctx.astype(LOW).reshape(seqs, length, heads, HEAD_DIM)
        grad_v = jnp.einsum("nhqk,nqhe->nkhe", probs, grad_ctx, preferred_element_type=F32)
        grad_probs = jnp.einsum("nqhe,nkhe->nhqk", grad_ctx, v, preferred_element_type=F32)
        probs_wide = probs.astype(F32)
        grad_scores = (
            probs_wide * (grad_probs - jnp.sum(probs_wide * grad_probs, axis=-1, keepdims=True))
        ).astype(LOW)
        grad_q = jnp.einsum("nhqk,nkhe->nqhe", grad_scores, k, preferred_element_type=F32) * factor
        grad_k = jnp.einsum("nhqk,nqhe->nkhe", grad_scores, q, preferred_element_type=F32) * factor
        grad_qkv = jnp.stack([grad_q, grad_k, grad_v], axis=2).astype(LOW).reshape(rows, edge)
        sums = jnp.sum(grad_qkv.astype(F32), axis=0)
        q_bias_part.append(sums[:head_cols])
        v_bias_part.append(sums[2 * head_cols :])
        g_qkv = dot_tn(act_one, grad_qkv).astype(LOW)
        g_att.append(jnp.concatenate([g_qkv, g_proj], axis=1))
        grad_act_one += dot_nt(grad_qkv, w_all[g, :, :edge]).astype(LOW).astype(F32)
    grad_inputs, clip_zero = squash_back(grad_act_one, bent_zero, ratio_zero)
    input_grad = lax.all_gather(
        (grad_one + grad_inputs).astype(LOW), "tensor", axis=0, tiled=True
    ).astype(F32)

    g_all = jnp.stack(
        [jnp.concatenate([g_att[g], g_up[g], g_down[g]], axis=1) for g in range(groups)]
    ).reshape(groups * parts, own_rows, 4 * head_cols + 2 * units)
    g_own = lax.psum_scatter(
        g_all, ("tensor", "dp"), scatter_dimension=0, tiled=False
    ).astype(F32)

    keep = jnp.abs(latents) < 1.0
    terms = jnp.where(keep, g_own[None] * scale_cols[:, None], 0.0)
    col_sums = jnp.sum(g_own[None] * signs, axis=1)
    ends = [0]
    for w in widths:
        ends.append(ends[-1] + w)
    scale_parts = jnp.stack([jnp.sum(col_sums[:, a:b], axis=1) for a, b in zip(ends[:-1], ends[1:])])

    clip_parts = jnp.stack([clip_zero, clip_one, clip_two, clip_three])
    small = jnp.concatenate(
        [
            jnp.concatenate(q_bias_part),
            jnp.concatenate(v_bias_part),
            jnp.concatenate(up_bias_part),
            proj_bias_part,
            down_bias_part,
            gain_one,
            gain_two,
            shift_one,
            shift_two,
            clip_parts,
            scale_parts.reshape(-1),
        ]
    )
    small = lax.psum(small, ("dp", "tensor"))
    pos = 0

    def take(n):
        nonlocal pos
        out = small[pos : pos + n]
        pos += n
        return out

    q_bias = lax.dynamic_slice_in_dim(take(groups * head_cols), group * head_cols, head_cols, 0)
    v_bias = lax.dynamic_slice_in_dim(take(groups * head_cols), group * head_cols, head_cols, 0)
    up_bias_grad = lax.dynamic_slice_in_dim(take(groups * units), group * units, units, 0)
    proj_bias_grad = take(model)
    down_bias_grad = take(model)
    gain_grad = take(2 * model).reshape(2, model)
    shift_grad = take(2 * model).reshape(2, model)
    clip_grad = take(4)
    scale_grad = take(12).reshape(6, 2)
    return (
        block_out,
        input_grad,
        terms[:, :, :edge].reshape(2, own_rows, 3, head_cols),
        jnp.stack([q_bias, v_bias]),
        terms[:, :, edge : edge + head_cols].transpose(0, 2, 1),
        proj_bias_grad,
        terms[:, :, start_up:start_down],
        up_bias_grad,
        terms[:, :, start_down:].transpose(0, 2, 1),
        down_bias_grad,
        gain_grad,
        shift_grad,
        clip_grad,
        scale_grad,
    )


def solution(mesh):
    return jax.shard_map(
        shards,
        mesh=mesh,
        in_specs=(
            P("dp", None),
            P("dp", None),
            P("dp", None),
            P(None, "dp", None, "tensor"),
            P(None, "tensor"),
            P(None, "tensor", "dp"),
            P(),
            P(None, "dp", "tensor"),
            P("tensor"),
            P(None, "tensor", "dp"),
            P(),
            P(),
            P(),
            P(),
            P(),
        ),
        out_specs=(
            P("dp", None),
            P("dp", None),
            P(None, "dp", None, "tensor"),
            P(None, "tensor"),
            P(None, "tensor", "dp"),
            P(),
            P(None, "dp", "tensor"),
            P("tensor"),
            P(None, "tensor", "dp"),
            P(),
            P(),
            P(),
            P(),
            P(),
        ),
        check_vma=False,
    )
```

time: 921 us -> 643 us (0.70)
  waiting for transfers between devices: 488 us -> 292 us
  other arithmetic: 116 us -> 42.8 us
  matrix products: 107 us -> 169 us
  local copies, waits for them, and re-layouts: 102 us -> 58.5 us
  blocking collectives: 82 us -> 55.1 us
    psum x4 -> x0, waiting for transfers between devices: 396 us -> none  [the longest x1 120 us: shards(): lax.psum(jnp.dot(act_four, w_down, preferred_element_type=jnp.float32).as...]
    reduce_scatter x1, waiting for transfers between devices: 55.2 us -> 162 us  [shards(): lax.psum_scatter(g_all, ('tensor', 'dp'), scatter_dimension=0, tiled=False)]
    all_gather x3, waiting for transfers between devices: 23.4 us -> 130 us  [the longest x1 88.9 us: shards(): w_all = lax.all_gather(w_own, ('tensor', 'dp'), axis=0, tiled=False)]
    dot_general x18 -> x68, matrix products: 107 us -> 156 us  [the longest x16 71.2 us: dot_nn(): lax.dot_general(a, b, (((1,), (0,)), ((), ())), preferred_element_type=F32)]
    reduce_sum x10 -> x7, other arithmetic: 44.1 us -> 5.84 us  [the longest x1 3.63 us: shards(): col_sums = jnp.sum(g_own[None] * signs, axis=1)]
    unnamed x121 -> x210, local copies, waits for them, and re-layouts: 57.3 us -> 21.9 us
    psum x2 -> x1, blocking collectives: 69.3 us -> 40 us  [shards(): small = lax.psum(small, ('dp', 'tensor'))]
    sub x0 -> x4, matrix products: none -> 13.8 us  [shards(): terms = jnp.exp(scores - top)]
  transfers between devices with their start and end apart: 11 -> 4, of which waited for: 8 -> 3; matrix products, arithmetic and copies ran while one was open for 26% -> 13% of each run, Pallas kernels for 0% -> 0%
where the time goes in v1:
time: 643 us; the launch traced here: 639 us
  waiting for transfers between devices  292 us (45%)
  matrix products  169 us (26%)
  local copies, waits for them, and re-layouts  58.5 us (9%)
  blocking collectives  55.1 us (9%)
  other arithmetic  42.8 us (7%)
  between operations  20.3 us (3%)
    reduce_scatter x1, waiting for transfers between devices, shards(): lax.psum_scatter(g_all, ('tensor', 'dp'), scatter_dimension=0, tiled=False)  162 us
    all_gather x1, waiting for transfers between devices, shards(): w_all = lax.all_gather(w_own, ('tensor', 'dp'), axis=0, tiled=False)  88.9 us
    dot_general x16, matrix products, dot_nn(): lax.dot_general(a, b, (((1,), (0,)), ((), ())), preferred_element_type=F32)  71.2 us
    all_gather x1, waiting for transfers between devices, shards(): lax.all_gather((grad_one + grad_inputs).astype(LOW), 'tensor', axis=0, ti...  41.1 us
    psum x1, blocking collectives, shards(): small = lax.psum(small, ('dp', 'tensor'))  40 us
    dot_general x16, matrix products, dot_nt(): lax.dot_general(a, b, (((1,), (1,)), ((), ())), preferred_element_type=F32)  31.5 us
    dot_general x16, matrix products, dot_tn(): lax.dot_general(a, b, (((0,), (0,)), ((), ())), preferred_element_type=F32)  29.3 us
    unnamed x210, local copies, waits for them, and re-layouts  21.9 us
  transfers between devices with their start and end apart: 4, of which 3 were waited for; matrix products, arithmetic and copies ran while one was open for 13% of the time, Pallas kernels for 0%

profile of v1, /device:TPU:0, one launch (start us, length us, event | category | flops | bytes accessed | tf_op | source)
XLA Modules:
  0.0 638.7 jit_solution(1430866692334760829)
XLA Ops:
  15.5 15.1 %all-gather.1 = f32[4,1,1152]{2,1,0:T(1,128)S(1)} all-gather(f32[1,1,1152]{2,1,0:T(1,128)S(1)} %reshape.879), channel_id=2, replica_groups=mesh['dp'=8,'tensor'=4] {'tensor'}, dimensions={0}, use_global_device_ids=true | all-gather | bytes 23040 | tf_op jit(solution)/shard_map/all_gather | solution.py:104
  31.8 88.9 %all-gather.6.cloned.1.call-done = bf16[32,96,2304]{2,1,0:T(8,128)(2,1)} async-done(((bf16[1,96,2304]{2,1,0:T(8,128)(2,1)}), bf16[32,96,2304]{2,1,0:T(8,128)(2,1)}) %all-gather.6.cloned.1.call-update) | async-done | bytes 14155792 | tf_op jit(solution)/shard_map/all_gather | solution.py:102
  120.7 3.9 fusion.57
  124.6 3.4 fusion.56
  128.0 2.5 fusion.55
  130.6 2.6 fusion.54
  133.2 2.9 fusion.130
  136.1 2.3 divide_convert_fusion.3
  141.8 2.9 fusion.129
  144.8 2.3 divide_convert_fusion.2
  150.6 4.0 fusion.128
  154.5 2.3 divide_convert_fusion.1
  156.9 2.7 multiply_convert_fusion.7
  159.6 2.5 convolution_convert_fusion.25
  162.1 4.0 fusion.131
  166.1 2.4 divide_convert_fusion
  170.1 2.2 fusion.132
  173.9 5.6 fusion.19
  179.7 9.8 %fusion.18 = (f32[512,768]{1,0:T(8,128)S(1)}, f32[512,768]{1,0:T(8,128)S(1)}) fusion(f32[768]{0:T(1024)S(1)} %get-tuple-element.101, bf16[512,768]{1,0:T(8,128)(2,1)S(1)} %multiply_convert_fusion.4, bf16[4,768,2304]{2,1,0:T(8,128)(2,1)S(1)} %bitcast.590), kind=kOutput, calls=%fused_computation.51 | convolution fusion | flops 628752384 | bytes 5115904 | tf_op jit(solution)/shard_map/dot_general | solution.py:12
  189.5 9.8 %fusion.17 = (f32[512,768]{1,0:T(8,128)S(1)}, f32[512,768]{1,0:T(8,128)S(1)}) fusion(f32[768]{0:T(1024)S(1)} %get-tuple-element.102, bf16[512,768]{1,0:T(8,128)(2,1)S(1)} %multiply_convert_fusion.4, bf16[4,768,2304]{2,1,0:T(8,128)(2,1)S(1)} %bitcast.591), kind=kOutput, calls=%fused_computation.50 | convolution fusion | flops 628752384 | bytes 5115904 | tf_op jit(solution)/shard_map/dot_general | solution.py:12
  199.3 10.0 %fusion.16 = (f32[512,768]{1,0:T(8,128)S(1)}, f32[512,768]{1,0:T(8,128)S(1)}) fusion(f32[768]{0:T(1024)S(1)} %get-tuple-element.99, bf16[512,768]{1,0:T(8,128)(2,1)S(1)} %multiply_convert_fusion.4, bf16[4,768,2304]{2,1,0:T(8,128)(2,1)S(1)} %bitcast.592), kind=kOutput, calls=%fused_computation.49 | convolution fusion | flops 628752384 | bytes 5115904 | tf_op jit(solution)/shard_map/dot_general | solution.py:12
  218.1 2.2 fusion.117
  220.4 3.0 convert_reduce_fusion
  223.4 3.0 convert_reduce_fusion.1
  226.5 3.0 convert_reduce_fusion.2
  229.5 3.4 convert_reduce_fusion.3
  235.5 3.4 multiply_reduce_fusion.8
  240.1 2.8 fusion.75
  247.9 2.8 fusion.78
  257.0 2.7 fusion.81
  266.3 2.8 fusion.84
  291.8 2.3 convolution_convert_fusion.8
  294.1 2.3 convolution_convert_fusion.9
  296.4 2.3 convolution_convert_fusion.10
  298.7 2.4 convolution_convert_fusion.11
  301.1 2.6 convolution_convert_fusion
  303.7 2.6 convolution_convert_fusion.2
  306.3 4.6 multiply_reduce_fusion.6
  312.7 2.4 convolution_convert_fusion.7
  323.5 6.6 %pad_maximum_fusion = bf16[4,768,2304]{1,2,0:T(8,128)(2,1)} fusion(bf16[1,768,2304]{1,2,0:T(8,128)(2,1)S(1)} %maximum_bitcast_fusion.3, bf16[1,768,2304]{1,2,0:T(8,128)(2,1)S(1)} %maximum_bitcast_fusion.2, bf16[1,768,2304]{1,2,0:T(8,128)(2,1)S(1)} %maximum_bitcast_fusion.1, bf16[1,768,2304]{1,2,0:T(8,128)(2,1)S(1)} %maximum_bitcast_fusion), kind=kLoop, calls=%fused_computation.4 | loop fusion | flops 21233664 | bytes 28311552 | tf_op jit(solution)/shard_map/stack | solution.py:219
  330.0 19.1 %copy.151 = bf16[4,768,2304]{2,1,0:T(8,128)(2,1)} copy(bf16[4,768,2304]{1,2,0:T(8,128)(2,1)} %pad_maximum_fusion) | data formatting | bytes 28311552 | tf_op jit(solution)/shard_map/stack | solution.py:219
  360.1 41.1 %all-gather.10.cloned.1.call-done = bf16[2048,768]{1,0:T(8,128)(2,1)} async-done(((bf16[512,768]{1,0:T(8,128)(2,1)}), bf16[2048,768]{1,0:T(8,128)(2,1)}) %all-gather.10.cloned.1.call-update) | async-done | bytes 3145744 | tf_op jit(solution)/shard_map/all_gather | solution.py:215
  401.2 5.1 convert_element_type.538
  406.3 162.0 %reduce-scatter.2.cloned.1.call-done = bf16[1,96,2304]{2,1,0:T(8,128)(2,1)} async-done(((bf16[32,96,2304]{2,1,0:T(8,128)(2,1)}), bf16[1,96,2304]{2,1,0:T(8,128)(2,1)}) %reduce-scatter.2.cloned.1.call-update) | async-done | bytes 442384 | tf_op jit(solution)/shard_map/reduce_scatter | solution.py:222
  569.8 3.6 multiply_reduce_fusion
  574.0 2.2 concatenate.91
  576.2 40.0 %psum.7 = f32[9232]{0:T(1024)S(1)} all-reduce(f32[9232]{0:T(1024)S(1)} %concatenate.91), channel_id=1, replica_groups=mesh['dp'=8,'tensor'=4] {'dp','tensor'}, use_global_device_ids=true, to_apply=%region_52.53 | all-reduce | flops 9232 | bytes 73856 | tf_op jit(solution)/shard_map/psum | solution.py:250
  622.3 2.4 copy.155
  (341 shorter events, 103.1 us)
Async XLA Ops:
  7.2 23.5 %copy-start = (s32[4,512]{1,0:T(4,128)S(1)}, s32[4,512]{1,0:T(4,128)}, u32[]{:S(2)}) copy-start(s32[4,512]{1,0:T(4,128)} %param.17) | copy-start | bytes 24580
  7.2 4.8 copy-start.47
  7.2 5.1 copy-start.46
  7.2 113.5 %all-gather.6.cloned.1.call-start = ((), (), s32[]{:S(2)}) async-start(), calls=%async_computation.1 | async-start | bytes 14598144 | tf_op jit(solution)/shard_map/all_gather | solution.py:102
  13.0 17.7 %copy-start.63 = (f32[4]{0:T(128)S(1)}, f32[4]{0:T(128)}, u32[]{:S(2)}) copy-start(f32[4]{0:T(128)} %param.28) | copy-start | bytes 52
  14.3 17.2 %copy-start.64 = (f32[2,768]{1,0:T(2,128)S(1)}, f32[2,768]{1,0:T(2,128)}, u32[]{:S(2)}) copy-start(f32[2,768]{1,0:T(2,128)} %param.27) | copy-start | bytes 18436
  14.3 17.2 %copy-start.65 = (f32[2,768]{1,0:T(2,128)S(1)}, f32[2,768]{1,0:T(2,128)}, u32[]{:S(2)}) copy-start(f32[2,768]{1,0:T(2,128)} %param.26) | copy-start | bytes 18436
  15.4 344.7 %all-gather.8.cloned.1.call-start = ((), (), s32[]{:S(2)}) async-start(), calls=%async_computation.2 | async-start | bytes 3932160 | tf_op jit(solution)/shard_map/all_gather | solution.py:157
  120.7 3.9 copy-start.50
  130.6 16.5 %copy-start.42 = (bf16[512,576]{0,1:T(8,128)(2,1)}, bf16[512,576]{0,1:T(8,128)(2,1)S(1)}, u32[]{:S(2)}) copy-start(bf16[512,576]{0,1:T(8,128)(2,1)S(1)} %fusion.55) | copy-start | bytes 1769476
  133.2 5.3 copy-start.40
  147.1 3.4 copy-start.2
  156.9 5.3 copy-start.4
  172.6 7.0 %slice-start = ((s8[14155776]{0:T(1024)(128)(4,1)}), s8[4194304]{0:T(1024)(128)(4,1)S(1)}, s32[]{:S(2)}) async-start(s8[14155776]{0:T(1024)(128)(4,1)} %bitcast.588), calls=%async_computation.5 | async-start | bytes 8388608
  173.9 113.9 %copy-start.25 = (bf16[512,768]{1,0:T(8,128)(2,1)}, bf16[512,768]{1,0:T(8,128)(2,1)S(1)}, u32[]{:S(2)}) copy-start(bf16[512,768]{1,0:T(8,128)(2,1)S(1)} %multiply_convert_fusion.4) | copy-start | bytes 2359300
  173.9 5.7 slice-start.1
  173.9 5.7 slice-start.2
  173.9 5.7 slice-start.3
  179.6 40.8 %copy-start.88 = (f32[512,768]{1,0:T(8,128)}, f32[512,768]{1,0:T(8,128)S(1)}, u32[]{:S(2)}) copy-start(f32[512,768]{1,0:T(8,128)S(1)} %get-tuple-element.209) | copy-start | bytes 4718596
  179.6 40.8 %copy-start.90 = (f32[512,768]{1,0:T(8,128)}, f32[512,768]{1,0:T(8,128)S(1)}, u32[]{:S(2)}) copy-start(f32[512,768]{1,0:T(8,128)S(1)} %get-tuple-element.210) | copy-start | bytes 4718596
  189.5 34.0 %copy-start.92 = (f32[512,768]{1,0:T(8,128)}, f32[512,768]{1,0:T(8,128)S(1)}, u32[]{:S(2)}) copy-start(f32[512,768]{1,0:T(8,128)S(1)} %get-tuple-element.211) | copy-start | bytes 4718596
  189.5 33.9 %copy-start.94 = (f32[512,768]{1,0:T(8,128)}, f32[512,768]{1,0:T(8,128)S(1)}, u32[]{:S(2)}) copy-start(f32[512,768]{1,0:T(8,128)S(1)} %get-tuple-element.212) | copy-start | bytes 4718596
  199.3 27.1 %copy-start.80 = (f32[512,768]{1,0:T(8,128)}, f32[512,768]{1,0:T(8,128)S(1)}, u32[]{:S(2)}) copy-start(f32[512,768]{1,0:T(8,128)S(1)} %get-tuple-element.213) | copy-start | bytes 4718596
  199.3 27.1 %copy-start.82 = (f32[512,768]{1,0:T(8,128)}, f32[512,768]{1,0:T(8,128)S(1)}, u32[]{:S(2)}) copy-start(f32[512,768]{1,0:T(8,128)S(1)} %get-tuple-element.214) | copy-start | bytes 4718596
  209.3 20.2 %copy-start.84 = (f32[512,768]{1,0:T(8,128)}, f32[512,768]{1,0:T(8,128)S(1)}, u32[]{:S(2)}) copy-start(f32[512,768]{1,0:T(8,128)S(1)} %get-tuple-element.215) | copy-start | bytes 4718596
  209.4 20.2 %copy-start.86 = (f32[512,768]{1,0:T(8,128)}, f32[512,768]{1,0:T(8,128)S(1)}, u32[]{:S(2)}) copy-start(f32[512,768]{1,0:T(8,128)S(1)} %get-tuple-element.216) | copy-start | bytes 4718596
  220.4 9.1 %copy-start.26 = (bf16[512,768]{1,0:T(8,128)(2,1)}, bf16[512,768]{1,0:T(8,128)(2,1)S(1)}, u32[]{:S(2)}) copy-start(bf16[512,768]{1,0:T(8,128)(2,1)S(1)} %convert_element_type.495) | copy-start | bytes 2359300
  223.4 9.5 %copy-start.74 = (bf16[512,768]{1,0:T(8,128)(2,1)}, bf16[512,768]{1,0:T(8,128)(2,1)S(1)}, u32[]{:S(2)}) copy-start(bf16[512,768]{1,0:T(8,128)(2,1)S(1)} %get-tuple-element.120) | copy-start | bytes 2359300
  226.5 7.3 %copy-start.76 = (bf16[512,768]{1,0:T(8,128)(2,1)}, bf16[512,768]{1,0:T(8,128)(2,1)S(1)}, u32[]{:S(2)}) copy-start(bf16[512,768]{1,0:T(8,128)(2,1)S(1)} %get-tuple-element.122) | copy-start | bytes 2359300
  229.5 5.1 copy-start.78
  240.0 2.9 copy-start.10
  246.8 3.9 copy-start.5
  247.9 4.1 copy-start.44
  256.0 3.8 copy-start.3
  257.0 4.0 copy-start.43
  266.3 4.1 copy-start.41
  275.5 125.7 %all-gather.10.cloned.1.call-start = ((), (), s32[]{:S(2)}) async-start(), calls=%async_computation.3 | async-start | bytes 3932160 | tf_op jit(solution)/shard_map/all_gather | solution.py:215
  276.3 2.9 copy-start.34
  276.3 2.9 copy-start.35
  276.3 2.9 copy-start.36
  301.1 2.6 copy-start.93
  311.0 257.3 %reduce-scatter.2.cloned.1.call-start = ((), (), s32[]{:S(2)}) async-start(), calls=%async_computation.4 | async-start | bytes 14598144 | tf_op jit(solution)/shard_map/reduce_scatter | solution.py:222
  311.3 3.8 copy-start.83
  569.8 4.2 copy-start.59
  569.8 4.2 copy-start.60
  569.8 4.2 copy-start.61
  569.8 4.2 copy-start.62
  622.3 8.0 %copy-start.14 = (bf16[2048,768]{1,0:T(8,128)(2,1)S(1)}, bf16[2048,768]{1,0:T(8,128)(2,1)}, u32[]{:S(2)}) copy-start(bf16[2048,768]{1,0:T(8,128)(2,1)} %all-gather.8.cloned.1.call-done) | copy-start | bytes 9437188
  (56 other events, 106.4 us)
Sparse Core Ops, SparseCore 0:
  15.5 105.2 all-gather.5
  275.6 61.8 all-gather.7
  339.1 62.0 all-gather.9
  407.1 161.2 reduce-scatter.1
